TPU v7x, 32 devices: a whole 2x2x4 slice. The times are simulated.
32 devices in a mesh: strip: 4 (over z), date: 8 (over y, x, core).
Axes of the slice: x: 2, y: 2, z: 4, core: 2. Of those that a mesh axis runs over, the one named last changes fastest.
Arguments:
- images: bfloat16 [128, 256, 128], P('date', 'strip'), may hold values from 0.19921875 to 5
- inverse_blocks: float32 [2, 8, 128, 128], P(None, 'strip', 'date'), as said below
- pair_first: int32 [256], P('date'), may hold values from 0 to 15
- pair_block: int32 [256, 1], P('date'), may hold values from 0 to 7; in each aligned block of 32 rows (0 to 31, 32 to 63, ...) at most 8 rows name the same one
- pair_second: int32 [256], P('date'), may hold values from 0 to 15
- pair_count: int32 [8], P('date'), may hold values from 8 to 32, as said below
- shifts: int32 [256, 2, 8], P('date', None, 'strip'), may hold values from -8 to 8
- anchors: int32 [8], P('strip'), may hold values from 0 to 96, as said below
Outputs:
- pair_offsets: float32 [256, 2, 8], P('date', None, 'strip')
- series: float32 [2, 8, 128], P(None, 'strip', 'date')
Inputs may be any that keep to these rules, and one draw needn't show every extreme that they name: `pair_block`: among the 32 slots of one date block at most 8 name one partner block, and some block is named that often. `pair_count`: slots 0 to count - 1 of a date block are live; slots at or past the count carry no pair, and their partner windows need not be sent. One block has all 32 live, one has 8, every other block 24 or more. `anchors`: chip q starts at column (q % 2) * 64 plus 0 to 32. `inverse_blocks`: symmetric in its last two dimensions.
All inputs are finite; a program needn't handle non-finite values.
Results may differ from a plain program's by a relative error of at most 0.008.
Values may be sent and summed in bfloat16 or wider, within the bound.
A program may use at most 64 MiB of HBM per device.

v0:
```python
import math

import jax
import jax.numpy as jnp
from jax import lax
from jax.sharding import PartitionSpec as P

SMAX = 8


def padded(cells, sides, width):
    for axis, dim in sides:
        count = lax.axis_size(axis)
        ends = count - 1
        head = lax.slice_in_dim(cells, 0, width, axis=dim)
        tail = lax.slice_in_dim(cells, cells.shape[dim] - width, cells.shape[dim], axis=dim)
        cells = jnp.concatenate(
            [
                lax.ppermute(tail, axis, [(i, (i + 1) % count) for i in range(ends)]),
                cells,
                lax.ppermute(head, axis, [((i + 1) % count, i) for i in range(ends)]),
            ],
            axis=dim,
        )
    return cells


def make_tables(length):
    counter = jnp.arange(length, dtype=jnp.int32)
    products = counter[:, None] * counter[None, :] % length
    radians = products.astype(jnp.float32) * (2.0 * math.pi / length)
    cosine = jnp.cos(radians)
    sine_part = -jnp.sin(radians)
    forward = jnp.concatenate([cosine, sine_part], axis=1).astype(jnp.bfloat16)
    over_len = 2 * length
    signed = jnp.where(counter < length // 2, counter, counter - length)
    places = jnp.arange(over_len, dtype=jnp.int32)
    turned = signed[:, None] * places[None, :] % over_len
    angles = turned.astype(jnp.float32) * (2.0 * math.pi / over_len)
    vcosine = jnp.cos(angles)
    vsine = jnp.sin(angles)
    top_rows = jnp.concatenate([vcosine, vsine], axis=1)
    low_rows = jnp.concatenate([-vsine, vcosine], axis=1)
    inverse_rows = jnp.concatenate([top_rows, low_rows], axis=0).astype(jnp.bfloat16)
    displace = ((places + length) % over_len - length).astype(jnp.float32) * 0.5
    return (
        forward,
        cosine.astype(jnp.bfloat16),
        sine_part.astype(jnp.bfloat16),
        inverse_rows,
        vcosine.T.astype(jnp.bfloat16),
        vsine.T.astype(jnp.bfloat16),
        displace,
    )


def spectra(windows, tables):
    forward, cosine_b, sine_b = (tables[0], tables[1], tables[2])
    length = windows.shape[-1]
    values = windows.astype(jnp.float32)
    centred = (values - jnp.mean(values, axis=(1, 2), keepdims=True)).astype(jnp.bfloat16)
    section_one = jnp.einsum(
        "bmn,nk->bmk", centred, forward, preferred_element_type=jnp.float32
    ).astype(jnp.bfloat16)
    with_cos = jnp.einsum("km,bmj->bkj", cosine_b, section_one, preferred_element_type=jnp.float32)
    with_sin = jnp.einsum("km,bmj->bkj", sine_b, section_one, preferred_element_type=jnp.float32)
    real_part = with_cos[:, :, :length] - with_sin[:, :, length:]
    imag_part = with_sin[:, :, :length] + with_cos[:, :, length:]
    return jnp.concatenate([real_part, imag_part], axis=2).astype(jnp.bfloat16)


def centroid(near_spec, far_spec, tables):
    inverse_rows, back_cos, back_sin, displace = (tables[3], tables[4], tables[5], tables[6])
    length = near_spec.shape[-1] // 2
    near_re = near_spec[:, :, :length].astype(jnp.float32)
    near_im = near_spec[:, :, length:].astype(jnp.float32)
    far_re = far_spec[:, :, :length].astype(jnp.float32)
    far_im = far_spec[:, :, length:].astype(jnp.float32)
    cross_re = near_re * far_re + near_im * far_im
    cross_im = near_im * far_re - near_re * far_im
    cross_spec = jnp.concatenate([cross_re, cross_im], axis=2).astype(jnp.bfloat16)
    along = jnp.einsum(
        "bun,nl->bul", cross_spec, inverse_rows, preferred_element_type=jnp.float32
    ).astype(jnp.bfloat16)
    half_width = along.shape[-1] // 2
    surface = jnp.einsum(
        "ku,bul->bkl", back_cos, along[:, :, :half_width], preferred_element_type=jnp.float32
    )
    surface = surface - jnp.einsum(
        "ku,bul->bkl", back_sin, along[:, :, half_width:], preferred_element_type=jnp.float32
    )
    energy = surface * surface
    norm_val = jnp.mean(energy, axis=(1, 2)) + 1e-06
    row_shift = jnp.mean(energy * displace[None, :, None], axis=(1, 2)) / norm_val
    col_shift = jnp.mean(energy * displace[None, None, :], axis=(1, 2)) / norm_val
    return jnp.stack([row_shift, col_shift], axis=1)


def body(images, inverse_blocks, pair_first, pair_block, pair_second, pair_count, shifts, anchors):
    devices = lax.axis_size("date")
    block_id = lax.axis_index("date")
    dates_dev, length, columns = images.shape
    pair_dev = pair_first.shape[0]
    chip_count = anchors.shape[0]
    capacity = max(2, 2 * pair_dev // devices)
    margin = SMAX
    extent = length + 2 * margin
    tables = make_tables(length)
    target = pair_block[:, 0]
    hit_table = (target[:, None] == jnp.arange(devices, dtype=jnp.int32)[None, :]).astype(jnp.int32)
    earlier = jnp.cumsum(hit_table, axis=0) - hit_table
    rank_in = jnp.sum(earlier * hit_table, axis=1)
    slot_of = target * capacity + rank_in
    requests = (
        jnp.zeros((devices * capacity,), jnp.int32)
        .at[slot_of]
        .set(pair_second)
        .reshape(devices, capacity)
    )
    asked_for = lax.all_to_all(requests, "date", split_axis=0, concat_axis=0, tiled=True)
    wanted = asked_for.reshape(-1)
    picked = jnp.take(images, wanted, axis=0).reshape(devices, capacity, length, columns)
    arrived = lax.all_to_all(picked, "date", split_axis=0, concat_axis=0, tiled=True)
    framed = padded(arrived, (("strip", 2),), margin)
    framed = framed.reshape(devices * capacity, extent, columns)
    framed = jnp.pad(framed, ((0, 0), (0, 0), (margin, margin + length // 2)))
    own_pad = jnp.pad(images, ((0, 0), (0, 0), (0, length // 2)))
    own_list = []
    region_list = []
    for chip_one in range(chip_count):
        own_list.append(lax.dynamic_slice_in_dim(own_pad, anchors[chip_one], length, 2))
        region_list.append(lax.dynamic_slice_in_dim(framed, anchors[chip_one], extent, 2))
    own_windows = jnp.stack(own_list, axis=1)
    regions = jnp.stack(region_list, axis=1)
    own_spec = spectra(own_windows.reshape(-1, length, length), tables).reshape(
        dates_dev, chip_count, length, 2 * length
    )
    step_pairs = math.gcd(pair_dev, max(1, 512 // chip_count))
    turn_count = pair_dev // step_pairs
    inside = jnp.arange(length, dtype=jnp.int32)
    across = jnp.arange(extent, dtype=jnp.int32)

    def one_turn(packed):
        slots_turn, firsts_turn, shifts_turn = packed
        regions_turn = jnp.take(regions, slots_turn, axis=0)
        row_start = margin + shifts_turn[:, 0, :]
        col_start = margin + shifts_turn[:, 1, :]
        row_pick = (
            across[None, None, None, :] == row_start[:, :, None, None] + inside[None, None, :, None]
        ).astype(jnp.bfloat16)
        col_pick = (
            across[None, None, :, None] == col_start[:, :, None, None] + inside[None, None, None, :]
        ).astype(jnp.bfloat16)
        row_cut = jnp.einsum(
            "pcie,pcef->pcif", row_pick, regions_turn, preferred_element_type=jnp.float32
        ).astype(jnp.bfloat16)
        far_windows = jnp.einsum(
            "pcif,pcfj->pcij", row_cut, col_pick, preferred_element_type=jnp.float32
        ).astype(jnp.bfloat16)
        far_spec = spectra(far_windows.reshape(-1, length, length), tables)
        near_spec = jnp.take(own_spec, firsts_turn, axis=0).reshape(-1, length, 2 * length)
        return centroid(near_spec, far_spec, tables).reshape(step_pairs, chip_count, 2)

    packed = (
        slot_of.reshape(turn_count, step_pairs),
        pair_first.reshape(turn_count, step_pairs),
        shifts.reshape(turn_count, step_pairs, 2, chip_count),
    )
    centroids = lax.map(one_turn, packed).reshape(pair_dev, chip_count, 2)
    live_mask = (jnp.arange(pair_dev, dtype=jnp.int32) < pair_count[0]).astype(jnp.float32)
    pair_offsets = (shifts.astype(jnp.float32) + jnp.swapaxes(centroids, 1, 2)) * live_mask[
        :, None, None
    ]
    dates_all = dates_dev * devices
    date_ids = jnp.arange(dates_all, dtype=jnp.int32)
    second_id = target * dates_dev + pair_second
    first_id = block_id * dates_dev + pair_first
    incidence = (second_id[:, None] == date_ids[None, :]).astype(jnp.float32) - (
        first_id[:, None] == date_ids[None, :]
    ).astype(jnp.float32)
    partial_value = jnp.einsum(
        "pxc,pd->xcd", pair_offsets, incidence, precision=lax.Precision.HIGHEST
    )
    rhs_whole = lax.psum(partial_value, "date")
    series = jnp.einsum("xcde,xce->xcd", inverse_blocks, rhs_whole, precision=lax.Precision.HIGHEST)
    return (pair_offsets, series)


def solution(mesh):
    return jax.shard_map(
        body,
        mesh=mesh,
        in_specs=(
            P("date", "strip", None),
            P(None, "strip", "date", None),
            P("date"),
            P("date", None),
            P("date"),
            P("date"),
            P("date", None, "strip"),
            P("strip"),
        ),
        out_specs=(P("date", None, "strip"), P(None, "strip", "date")),
        check_vma=False,
    )
```

profile of v0, /device:TPU:0, one launch (start us, length us, event | category | flops | bytes accessed | tf_op | source)
XLA Modules:
  0.0 84.8 jit_solution(15809964024096351249)
XLA Ops:
  0.6 0.0 copy-start
  0.6 0.7 fusion.76
  1.4 0.1 reduce_window_sum.11
  1.4 0.8 select_reduce_fusion
  2.3 0.7 and_bitcast_fusion
  2.9 0.8 scatter_custom_fusion
  3.7 0.7 all_to_all.9
  4.4 5.2 %all-to-all-start = ((s32[8,1,8]{2,1,0:T(1,128)}), s32[8,1,8]{2,1,0:T(1,128)S(1)}, u32[]{:S(2)}, u32[]{:S(2)}) async-start(s32[8,1,8]{2,1,0:T(1,128)} %bitcast.18), calls=%async_computation | async-start | bytes 8192 | tf_op jit(solution)/shard_map/all_to_all | solution.py:120
  9.6 0.2 negate_convert_fusion.1
  9.8 1.3 %fusion.120 = (s32[1]{0:T(128)}, s32[1]{0:T(128)}) fusion(s32[2]{0:T(128)} %param.15), kind=kLoop, calls=%fused_computation.195 | loop fusion | bytes 16 | tf_op jit(solution)/shard_map/slice | solution.py:132
  15.0 1.3 %fusion.32 = (bf16[16,1,64,64]{3,2,1,0:T(8,128)(2,1)S(1)}, bf16[16,1,64,64]{3,2,1,0:T(8,128)(2,1)S(1)}) fusion(s32[]{:T(128)S(6)} %select_n.129, bf16[16,64,128]{2,1,0:T(8,128)(2,1)} %param.8, s32[]{:T(128)S(6)} %select_n.130), kind=kLoop, calls=%fused_computation.64 | loop fusion | bytes 524296 | tf_op jit(solution)/shard_map/stack | solution.py:133
  16.2 0.1 maximum_convert_fusion
  16.4 0.2 fusion.34
  16.6 0.1 div.58
  16.7 0.2 fusion.26
  16.9 0.0 copy-start.2
  16.9 0.3 convolution_convert_fusion.2
  17.3 0.4 convolution_bitcast_fusion.2
  17.7 0.4 convolution_bitcast_fusion.3
  18.1 0.1 copy.19
  18.2 0.1 copy.21
  18.3 0.6 fusion.22
  19.0 0.0 copy-start.1
  19.0 0.3 pad_maximum_fusion.2
  19.3 0.1 broadcast_in_dim.83
  19.3 0.1 broadcast_in_dim.84
  20.1 0.7 gather_fusion
  20.9 0.6 broadcast.369
  21.5 0.7 reduce.8
  22.2 0.1 reshape.257
  22.3 0.7 gather_fusion.1
  23.1 0.0 copy-start.3
  23.1 1.2 %broadcast_select_fusion = bf16[8,8,64,128]{3,2,1,0:T(8,128)(2,1)} fusion(bf16[8,8,64,128]{3,2,1,0:T(8,128)(2,1)S(1)} %bitcast.101, pred[8,8]{1,0:T(8,128)(4,1)S(1)} %compare_and_fusion), kind=kLoop, calls=%fused_computation.58 | loop fusion | flops 524288 | bytes 2097216 | tf_op jit(solution)/shard_map/jit(_take)/select_n | solution.py:122
  24.2 4.2 %all-to-all-start.1 = ((bf16[8,8,64,128]{3,2,1,0:T(8,128)(2,1)}), bf16[8,8,64,128]{3,2,1,0:T(8,128)(2,1)S(1)}, u32[]{:S(2)}, u32[]{:S(2)}) async-start(bf16[8,8,64,128]{3,2,1,0:T(8,128)(2,1)} %broadcast_select_fusion), calls=%async_computation.1 | async-start | bytes 2097152 | tf_op jit(solution)/shard_map/all_to_all | solution.py:123
  28.5 0.2 fusion.75
  28.7 0.1 iota_add_fusion
  28.8 0.2 bitcast_select_fusion
  29.1 14.8 %all-to-all-done.1 = bf16[8,8,64,128]{3,2,1,0:T(8,128)(2,1)S(1)} async-done(((bf16[8,8,64,128]{3,2,1,0:T(8,128)(2,1)}), bf16[8,8,64,128]{3,2,1,0:T(8,128)(2,1)S(1)}, u32[]{:S(2)}, u32[]{:S(2)}) %all-to-all-start.1) | async-done | bytes 1048608 | tf_op jit(solution)/shard_map/all_to_all | solution.py:123
  43.8 0.1 fusion.119
  43.9 3.5 %collective-permute-start = (bf16[8,8,8,128]{3,2,1,0:T(8,128)(2,1)S(1)}, bf16[8,8,8,128]{3,2,1,0:T(8,128)(2,1)S(1)}, u32[]{:S(2)}, u32[]{:S(2)}) collective-permute-start(bf16[8,8,8,128]{3,2,1,0:T(8,128)(2,1)S(1)} %get-tuple-element.68), channel_id=1, source_target_pairs={{0,8},{8,16},{16,24},{1,9},{9,17},{17,25},{2,10},{10,18},{18,26},{... | collective-permute-start | bytes 393224 | tf_op jit(solution)/shard_map/ppermute | solution.py:19
  47.4 1.5 %collective-permute-start.1 = (bf16[8,8,8,128]{3,2,1,0:T(8,128)(2,1)S(1)}, bf16[8,8,8,128]{3,2,1,0:T(8,128)(2,1)S(1)}, u32[]{:S(2)}, u32[]{:S(2)}) collective-permute-start(bf16[8,8,8,128]{3,2,1,0:T(8,128)(2,1)S(1)} %get-tuple-element.69), channel_id=1, source_target_pairs={{8,0},{16,8},{24,16},{9,1},{17,9},{25,17},{10,2},{18,10},{26,18},{... | collective-permute-start | bytes 393224 | tf_op jit(solution)/shard_map/ppermute | solution.py:21
  51.5 2.8 %collective-permute-done.1 = bf16[8,8,8,128]{3,2,1,0:T(8,128)(2,1)S(1)} collective-permute-done((bf16[8,8,8,128]{3,2,1,0:T(8,128)(2,1)S(1)}, bf16[8,8,8,128]{3,2,1,0:T(8,128)(2,1)S(1)}, u32[]{:S(2)}, u32[]{:S(2)}) %collective-permute-start.1) | collective-permute-done | bytes 131104 | tf_op jit(solution)/shard_map/ppermute | solution.py:21
  54.3 0.2 pad_maximum_fusion.1
  54.4 1.1 %fusion.12 = (bf16[64,1,80,80]{3,2,0,1:T(8,128)(2,1)S(1)}, bf16[64,1,80,80]{3,2,0,1:T(8,128)(2,1)S(1)}) fusion(s32[]{:T(128)S(6)} %select_n.137, bf16[64,80,128]{2,1,0:T(8,128)(2,1)S(1)} %bitcast.100, s32[]{:T(128)S(6)} %select_n.138), kind=kLoop, calls=%fused_computation.37 | loop fusion | bytes 2949128 | tf_op jit(solution)/shard_map/stack | solution.py:134
  55.5 2.1 %pad_maximum_fusion = bf16[64,2,80,80]{3,2,0,1:T(8,128)(2,1)} fusion(bf16[64,1,80,80]{3,2,0,1:T(8,128)(2,1)S(1)} %get-tuple-element.67, bf16[64,1,80,80]{3,2,0,1:T(8,128)(2,1)S(1)} %get-tuple-element.66), kind=kLoop, calls=%fused_computation.13 | loop fusion | flops 819200 | bytes 3276800 | tf_op jit(solution)/shard_map/stack | solution.py:134
  57.6 3.5 %gather_fusion.2 = bf16[32,2,80,80]{3,2,1,0:T(8,128)(2,1)} fusion(bf16[64,2,80,80]{3,2,0,1:T(8,128)(2,1)} %pad_maximum_fusion, s32[1024]{0:T(1024)S(1)} %pad_clamp_fusion), kind=kCustom, calls=%fused_computation.2 | custom fusion | bytes 1638528 | tf_op jit(solution)/shard_map/while/body/eval_jaxpr/jit(_take)/gather | solution.py:145
  61.1 2.8 %fusion.121 = (f32[32,2]{1,0:T(8,128)S(1)}, f32[32,2,64,64]{3,2,1,0:T(8,128)S(1)}) fusion(s32[32,2,64]{2,1,0:T(2,128)S(1)} %get-tuple-element.87, bf16[32,2,80,80]{3,2,1,0:T(8,128)(2,1)} %gather_fusion.2, pred[32]{0:T(512)(128)(4,1)S(1)} %get-tuple-element.46, s32[32,2,64]{2,1,0:T(2,128)S(1)} %get-tuple-element.88), kind=kOutput, calls=%fused_computation.196 | convolution fusion | flops 96550848 | bytes 1900832 | tf_op jit(solution)/shard_map/while/body/eval_jaxpr/pcif,pcfj->pcij/dot_general | solution.py:157
  63.9 0.1 div.60
  64.0 0.2 fusion.6
  64.3 0.5 convolution_convert_fusion.1
  64.7 0.5 convolution_bitcast_fusion
  65.3 0.5 convolution_bitcast_fusion.1
  65.8 1.5 %fusion.1 = (bf16[64,64,64]{2,1,0:T(8,128)(2,1)S(1)}, bf16[64,64,64]{2,1,0:T(8,128)(2,1)S(1)}, bf16[64,64,64]{2,1,0:T(8,128)(2,1)S(1)}) fusion(bf16[64,64,128]{2,1,0:T(8,128)(2,1)S(1)} %bitcast_select_fusion, f32[64,64,128]{2,1,0:T(8,128)S(1)} %convolution_bitcast_fusion.1, f32[64,64,128]{2,1,0:T(8,128)S(1)} %convolution_bitcast_fusion), kind=kLoop, calls=%fused_computation.15 | loop fusion | flops 3145728 | bytes 6815744 | tf_op jit(solution)/shard_map/convert.8
  67.3 0.8 fusion.3
  68.1 0.8 convolution_convert_fusion
  68.9 0.9 %fusion.19 = f32[64,128,128]{2,1,0:T(8,128)S(1)} fusion(bf16[64,64,256]{2,1,0:T(8,128)(2,1)S(1)} %convolution_convert_fusion, s32[64]{0:T(128)S(1)} %compare_select_fusion.1), kind=kOutput, calls=%fused_computation.44 | convolution fusion | flops 134340608 | bytes 5243392 | tf_op jit(solution)/shard_map/while/body/eval_jaxpr/ku,bul->bkl/dot_general | solution.py:86
  69.8 1.9 %multiply_reduce_fusion.1 = (f32[64]{0:T(128)S(1)}, f32[64]{0:T(128)S(1)}, f32[64]{0:T(128)S(1)}) fusion(f32[128]{0:T(128)S(1)} %fusion.89, f32[64,128,128]{2,1,0:T(8,128)S(1)} %fusion.19, s32[64]{0:T(128)S(1)} %compare_select_fusion.1, bf16[64,64,256]{2,1,0:T(8,128)(2,1)S(1)} %convolution_convert_fusion), kind=kOutput, calls=%fused_computation.5 | convolution fusion | flops 141680448 | bytes 5245184 | tf_op jit(solution)/shard_map/while/body/eval_jaxpr/ku,bul->bkl/dot_general | solution.py:89
  71.6 0.1 div.64
  71.8 0.1 copy.22
  71.8 0.1 div.67
  71.9 0.1 copy.23
  72.1 0.2 fusion.63
  72.3 11.8 %psum.7 = f32[2,2,128]{2,1,0:T(2,128)S(1)} all-reduce(f32[2,2,128]{2,1,0:T(2,128)S(1)} %fusion.63), channel_id=1, replica_groups=mesh['strip'=4,'date'=8] {'date'}, use_global_device_ids=true, to_apply=%region_8.9 | all-reduce | flops 512 | bytes 4096 | tf_op jit(solution)/shard_map/psum | solution.py:184
  84.1 0.7 fusion.124
  (29 shorter events, 0.1 us)
Async XLA Ops:
  0.6 83.5 %copy-start = (f32[2,2,16,128]{3,2,1,0:T(8,128)S(1)}, f32[2,2,16,128]{3,2,1,0:T(8,128)}, u32[]{:S(2)}) copy-start(f32[2,2,16,128]{3,2,1,0:T(8,128)} %param.9) | copy-start | bytes 98308
  4.4 16.4 %all-to-all-start = ((s32[8,1,8]{2,1,0:T(1,128)}), s32[8,1,8]{2,1,0:T(1,128)S(1)}, u32[]{:S(2)}, u32[]{:S(2)}) async-start(s32[8,1,8]{2,1,0:T(1,128)} %bitcast.18), calls=%async_computation | async-start | bytes 8192 | tf_op jit(solution)/shard_map/all_to_all | solution.py:120
  16.9 1.2 %copy-start.2 = (s32[32,2,2]{0,2,1:T(2,128)S(1)}, s32[32,2,2]{0,2,1:T(2,128)}, u32[]{:S(2)}) copy-start(s32[32,2,2]{0,2,1:T(2,128)} %param.14) | copy-start | bytes 1540
  16.9 1.4 %copy-start.5 = (s32[32]{0:T(128)S(1)}, s32[32]{0:T(128)}, u32[]{:S(2)}) copy-start(s32[32]{0:T(128)} %param.10) | copy-start | bytes 388
  19.0 3.3 %copy-start.1 = (bf16[16,64,128]{2,1,0:T(8,128)(2,1)S(1)}, bf16[16,64,128]{2,1,0:T(8,128)(2,1)}, u32[]{:S(2)}) copy-start(bf16[16,64,128]{2,1,0:T(8,128)(2,1)} %param.8) | copy-start | bytes 786436
  23.1 5.4 %copy-start.3 = (s32[32,1]{0,1:T(1,128)S(1)}, s32[32,1]{0,1:T(1,128)}, u32[]{:S(2)}) copy-start(s32[32,1]{0,1:T(1,128)} %param.11) | copy-start | bytes 388
  23.1 5.4 %copy-start.6 = (s32[32]{0:T(128)S(1)}, s32[32]{0:T(128)}, u32[]{:S(2)}) copy-start(s32[32]{0:T(128)} %param.12) | copy-start | bytes 388
  24.2 19.6 %all-to-all-start.1 = ((bf16[8,8,64,128]{3,2,1,0:T(8,128)(2,1)}), bf16[8,8,64,128]{3,2,1,0:T(8,128)(2,1)S(1)}, u32[]{:S(2)}, u32[]{:S(2)}) async-start(bf16[8,8,64,128]{3,2,1,0:T(8,128)(2,1)} %broadcast_select_fusion), calls=%async_computation.1 | async-start | bytes 2097152 | tf_op jit(solution)/shard_map/all_to_all | solution.py:123
  43.9 7.6 %collective-permute-start = (bf16[8,8,8,128]{3,2,1,0:T(8,128)(2,1)S(1)}, bf16[8,8,8,128]{3,2,1,0:T(8,128)(2,1)S(1)}, u32[]{:S(2)}, u32[]{:S(2)}) collective-permute-start(bf16[8,8,8,128]{3,2,1,0:T(8,128)(2,1)S(1)} %get-tuple-element.68), channel_id=1, source_target_pairs={{0,8},{8,16},{16,24},{1,9},{9,17},{17,25},{2,10},{10,18},{18,26},{... | collective-permute-start | bytes 393224 | tf_op jit(solution)/shard_map/ppermute | solution.py:19
  47.4 6.9 %collective-permute-start.1 = (bf16[8,8,8,128]{3,2,1,0:T(8,128)(2,1)S(1)}, bf16[8,8,8,128]{3,2,1,0:T(8,128)(2,1)S(1)}, u32[]{:S(2)}, u32[]{:S(2)}) collective-permute-start(bf16[8,8,8,128]{3,2,1,0:T(8,128)(2,1)S(1)} %get-tuple-element.69), channel_id=1, source_target_pairs={{8,0},{16,8},{24,16},{9,1},{17,9},{25,17},{10,2},{18,10},{26,18},{... | collective-permute-start | bytes 393224 | tf_op jit(solution)/shard_map/ppermute | solution.py:21
  72.1 12.8 %copy-start.4 = (f32[32,2,2]{0,2,1:T(2,128)}, f32[32,2,2]{0,2,1:T(2,128)S(1)}, u32[]{:S(2)}) copy-start(f32[32,2,2]{0,2,1:T(2,128)S(1)} %copy.25) | copy-start | bytes 1540
where the time goes:
time: 85.4 us; the launch traced here: 84.8 us
  waiting for transfers between devices  17.5 us (20%)
  starting transfers between devices  14.4 us (17%)
  local copies, waits for them, and re-layouts  11.9 us (14%)
  blocking collectives  11.8 us (14%)
  other arithmetic  11.2 us (13%)
  matrix products  9.92 us (12%)
  between operations  8.17 us (10%)
    all_to_all x1, waiting for transfers between devices, body(): lax.all_to_all(picked, 'date', split_axis=0, concat_axis=0, tiled=True)  14.8 us
    psum x1, blocking collectives, body(): rhs_whole = lax.psum(partial_value, 'date')  11.8 us
    all_to_all x1, starting transfers between devices, body(): lax.all_to_all(requests, 'date', split_axis=0, concat_axis=0, tiled=True)  5.2 us
    all_to_all x1, starting transfers between devices, body(): lax.all_to_all(picked, 'date', split_axis=0, concat_axis=0, tiled=True)  4.2 us
    gather x1, local copies, waits for them, and re-layouts, one_turn(): regions_turn = jnp.take(regions, slots_turn, axis=0)  3.54 us
    ppermute x1, starting transfers between devices, padded(): lax.ppermute(tail, axis, [(i, (i + 1) % count) for i in range(ends)])  3.49 us
    another operation x5, other arithmetic  3.26 us
    ppermute x1, waiting for transfers between devices, padded(): lax.ppermute(head, axis, [((i + 1) % count, i) for i in range(ends)])  2.76 us
  transfers between devices with their start and end apart: 4, of which 2 were waited for; matrix products, arithmetic and copies ran while one was open for 8% of the time, Pallas kernels for 0%

commit v1 on v0

v1 whole, which is shorter than its diff:
```python
import functools
import math

import jax
import jax.numpy as jnp
import numpy as np
from jax import lax
from jax.experimental import pallas as pl
from jax.experimental.pallas import tpu as pltpu
from jax.sharding import PartitionSpec as P

SMAX = 8
MESH = pl.DeviceIdType.MESH
F32, BF16 = jnp.float32, jnp.bfloat16


def make_tables(length):
    counter = np.arange(length)
    radians = (counter[:, None] * counter[None, :] % length) * (2.0 * math.pi / length)
    cosine, sine = np.cos(radians), -np.sin(radians)
    over = 2 * length
    signed = np.where(counter < length // 2, counter, counter - length)
    places = np.arange(over)
    angles = (signed[:, None] * places[None, :] % over) * (2.0 * math.pi / over)
    vcos, vsin = np.cos(angles), np.sin(angles)
    forward = np.concatenate([cosine, sine, -sine, cosine], axis=1)
    forward = np.concatenate([forward, np.zeros_like(forward)], axis=0)
    rows = np.concatenate([cosine, sine], axis=1)
    one = np.concatenate([vcos, vsin], axis=1)
    two = np.concatenate([-vsin, vcos], axis=1)
    back = np.concatenate([one, one, two, -two], axis=0)
    final = np.concatenate([vcos.T, -vsin.T], axis=1)
    return [jnp.asarray(t.astype(np.float32)).astype(BF16) for t in (forward, rows, back, final)]


def gather_kernel(n, strips, img, top, bot, grid_out, halo_out, local, send, recv):
    me = lax.axis_index("date")
    strip = lax.axis_index("strip")
    up, down = lax.rem(strip + strips - 1, strips), lax.rem(strip + 1, strips)
    half = img.shape[0] // 2
    first, second = pl.ds(0, half), pl.ds(half, img.shape[0] - half)

    def sent(k, src, dst, where):
        return pltpu.make_async_remote_copy(
            src_ref=src,
            dst_ref=dst,
            send_sem=send.at[k],
            recv_sem=recv.at[k],
            device_id=where,
            device_id_type=MESH,
        )

    hier = n == 8
    if hier:
        steps = [1, 2, 4]
        peers = [jnp.bitwise_xor(me, j) for j in steps]
    else:
        peers = [lax.rem(me + j, n) for j in range(1, n)]
    barrier = pltpu.get_barrier_semaphore()
    for peer in peers:
        pl.semaphore_signal(barrier, inc=1, device_id={"date": peer}, device_id_type=MESH)
    for other in (up, down):
        pl.semaphore_signal(barrier, inc=1, device_id={"strip": other}, device_id_type=MESH)
    own = pltpu.make_async_copy(img, grid_out.at[me], local.at[0])
    own.start()
    pl.semaphore_wait(barrier, len(peers) + 2)

    z_up = sent(0, top, halo_out.at[me, 0], {"strip": up})
    z_down = sent(1, bot, halo_out.at[me, 1], {"strip": down})
    if not hier:
        z_up.start()
        z_down.start()
        mains = []
        for j, peer in enumerate(peers):
            mains.append(sent(2 + j, img, grid_out.at[me], {"date": peer}))
            mains[-1].start()
        z_up.wait()
        z_down.wait()
        for j, peer in enumerate(peers):
            mains.append(sent(n + 1 + j, halo_out.at[me], halo_out.at[me], {"date": peer}))
            mains[-1].start()
        for copy in mains:
            copy.wait()
        own.wait()
        return

    core, ex, wy = ({"date": peer} for peer in peers)

    def family(base, own_ref, out, one, two):
        def made(k, block, part, where, mine=False):
            src = own_ref.at[part] if mine else out.at[block, part]
            return sent(base + k, src, out.at[block, part], where)

        near_x, near_y, diag = (jnp.bitwise_xor(me, j) for j in (2, 4, 6))
        return [
            made(0, me, one, wy, True),
            made(1, me, two, wy, True),
            made(2, me, two, ex, True),
            made(3, me, one, ex, True),
            made(4, me, one, core, True),
            made(5, near_y, one, ex),
            made(6, near_y, one, core),
            made(7, near_x, two, wy),
            made(8, near_x, two, core),
            made(9, near_y, two, core),
            made(10, near_x, one, core),
            made(11, diag, one, core),
            made(12, diag, two, core),
            made(13, me, two, core, True),
        ]

    main = family(2, img, grid_out, first, second)
    halo = family(16, halo_out.at[me], halo_out, 0, 1)

    def run(copies, ids):
        for k in ids:
            copies[k].start()

    run(main, (0, 2))
    z_up.start()
    z_down.start()
    run(main, (1, 3, 4, 13))
    main[0].wait_recv()
    run(main, (5, 6))
    main[2].wait_recv()
    run(main, (7, 8))
    z_up.wait_recv()
    z_down.wait_recv()
    run(halo, (0, 2, 1, 3, 4, 13))
    main[1].wait_recv()
    run(main, (9,))
    main[3].wait_recv()
    run(main, (10,))
    main[5].wait_recv()
    run(main, (11,))
    main[7].wait_recv()
    run(main, (12,))
    halo[0].wait_recv()
    run(halo, (5, 6))
    halo[2].wait_recv()
    run(halo, (7, 8))
    halo[1].wait_recv()
    run(halo, (9,))
    halo[3].wait_recv()
    run(halo, (10,))
    halo[5].wait_recv()
    run(halo, (11,))
    halo[7].wait_recv()
    run(halo, (12,))
    for k in (4, 13, 6, 8, 9, 10, 11, 12):
        main[k].wait_recv()
        halo[k].wait_recv()
    for copy in main + halo + [z_up, z_down]:
        copy.wait_send()
    own.wait()


def pairs_kernel(
    n, strips, batch,
    first_s, block_s, second_s, count_s, shifts_s, anchors_s,
    img, grid_in, halo_in, forward, rows, back, final,
    offsets_out, partial_out,
    wide, far, near, spec, sums, moments, moves,
):
    dates, length, cols = img.shape
    pairs, chips = first_s.shape[0], anchors_s.shape[0]
    me, strip = lax.axis_index("date"), lax.axis_index("strip")
    lane = lax.broadcasted_iota(jnp.int32, (length, cols), 1)
    has_up, has_down = strip > 0, strip < strips - 1
    half_dates = dates // 2

    def turned(value, start):
        rolled = pltpu.roll(value, lax.rem(2 * cols - start, cols), 1)
        inside = (lane >= -start) & (lane < cols - start)
        return jnp.where(inside, rolled, 0.0).astype(BF16)

    def near_cut(d, carry):
        value = img[d].astype(F32)
        for c in range(chips):
            near[d * chips + c] = turned(value, anchors_s[c])
        return carry

    lax.fori_loop(0, dates, near_cut, 0, unroll=4)

    def far_cut(p, carry):
        block, day = block_s[p], second_s[p]
        wide[p, pl.ds(SMAX, length)] = grid_in[block * dates + day].astype(F32)
        odd = lax.rem(day, 2) == 1
        tile = block * dates + day // 2
        for side, at, has in ((0, SMAX + length, has_down), (1, 0, has_up)):
            held = halo_in[tile + side * half_dates].astype(F32)
            edge = jnp.where(odd, held[SMAX:], held[:SMAX])
            wide[p, pl.ds(at, SMAX)] = jnp.where(has, edge, 0.0)
        for c in range(chips):
            value = wide[p, pl.ds(SMAX + shifts_s[0, c, p], length)]
            far[p * chips + c] = turned(value, anchors_s[c] + shifts_s[1, c, p])
        place = lax.broadcasted_iota(jnp.int32, (1, cols), 1)
        row = jnp.zeros((1, cols), F32)
        for x in range(2):
            for c in range(chips):
                row = jnp.where(place == x * chips + c, shifts_s[x, c, p].astype(F32), row)
        row = jnp.where(place == 2 * chips, (block * dates + day).astype(F32), row)
        row = jnp.where(place == 2 * chips + 1, (me * dates + first_s[p]).astype(F32), row)
        moves[pl.ds(p, 1)] = row
        return carry

    lax.fori_loop(0, pairs, far_cut, 0, unroll=4)

    width = 2 * length
    lanes2 = lax.broadcasted_iota(jnp.int32, (1, 2 * width), 1)
    base = jnp.where((lanes2 == 0) | (lanes2 == width + length), 1.0 / length, 0.0)

    def spectra(ref, at, many):
        windows = ref[pl.ds(at, many)].reshape(many * length, cols)
        section = jnp.dot(windows, forward[...], preferred_element_type=F32)
        stacked = []
        for w in range(many):
            part = section[w * length:(w + 1) * length]
            part = (part - jnp.sum(part, axis=0, keepdims=True) * base).astype(BF16)
            stacked.append(jnp.concatenate([part[:, :width], part[:, width:]], axis=0))
        return jnp.dot(
            rows[...], jnp.concatenate(stacked, axis=1), preferred_element_type=F32
        )

    many = batch * chips

    def near_turn(t, carry):
        found = spectra(near, t * many, many)
        for w in range(many):
            value = found[:, w * width:(w + 1) * width]
            both = jnp.concatenate([value, pltpu.roll(value, length, 1)], axis=1)
            spec[t * many + w] = both.astype(BF16)
        return carry

    lax.fori_loop(0, dates // batch, near_turn, 0)

    steps = lax.broadcasted_iota(jnp.int32, (width, 1), 0)
    down_k = jnp.where(steps < length, steps, steps - width).astype(F32) * 0.5
    down_k = jnp.broadcast_to(down_k, (width, width))

    def turn(t, carry):
        found = spectra(far, t * many, many).astype(BF16)
        crossed = []
        for b in range(batch):
            day = first_s[t * batch + b]
            for c in range(chips):
                w = b * chips + c
                value = found[:, w * width:(w + 1) * width]
                crossed.append(spec[day * chips + c] * jnp.concatenate([value, value], axis=1))
        along = jnp.dot(
            jnp.concatenate(crossed, axis=0), back[...], preferred_element_type=F32
        ).astype(BF16)
        stacked = []
        for w in range(many):
            part = along[w * length:(w + 1) * length]
            stacked.append(jnp.concatenate([part[:, :width], part[:, width:]], axis=0))
        surface = jnp.dot(
            final[...], jnp.concatenate(stacked, axis=1), preferred_element_type=F32
        )
        for b in range(batch):
            for c in range(chips):
                w = b * chips + c
                value = surface[:, w * width:(w + 1) * width]
                energy = value * value
                at = (c, pl.ds(t * batch + b, 1))
                sums[at] = jnp.sum(energy, axis=0, keepdims=True)
                moments[at] = jnp.sum(energy * down_k, axis=0, keepdims=True)
        return carry

    lax.fori_loop(0, pairs // batch, turn, 0)

    across = lax.broadcasted_iota(jnp.int32, (pairs, width), 1)
    across = jnp.where(across < length, across, across - width).astype(F32) * 0.5
    live = lax.broadcasted_iota(jnp.int32, (pairs, 1), 0) < count_s[0]
    cells = 1.0 / (width * width)
    shift_all = moves[...]
    spot = lax.broadcasted_iota(jnp.int32, (pairs, partial_out.shape[1]), 1).astype(F32)
    spread = (spot == shift_all[:, 2 * chips:2 * chips + 1]).astype(F32) - (
        spot == shift_all[:, 2 * chips + 1:2 * chips + 2]
    ).astype(F32)
    columns = [None] * (2 * chips)
    for c in range(chips):
        held = sums[c]
        scale = jnp.sum(held, axis=1, keepdims=True) * cells + 1e-6
        low = jnp.sum(moments[c], axis=1, keepdims=True) * cells
        side = jnp.sum(held * across, axis=1, keepdims=True) * cells
        for x, value in enumerate((low, side)):
            k = x * chips + c
            columns[k] = jnp.where(live, shift_all[:, k:k + 1] + value / scale, 0.0)
    place = lax.broadcasted_iota(jnp.int32, (pairs, width), 1)
    table = jnp.zeros((pairs, width), F32)
    for k, column in enumerate(columns):
        table = jnp.where(place == k, column, table)
        partial_out[k:k + 1] = jnp.sum(column * spread, axis=0, keepdims=True)
    turned_table = jnp.transpose(table)
    for x in range(2):
        offsets_out[x] = turned_table[x * chips:(x + 1) * chips]


def series_kernel(n, partial, inverse, series_out, held, send, recv):
    me = lax.axis_index("date")
    peers = [lax.rem(me + j, n) for j in range(1, n)]
    barrier = pltpu.get_barrier_semaphore()
    for peer in peers:
        pl.semaphore_signal(barrier, inc=1, device_id={"date": peer}, device_id_type=MESH)
    pl.semaphore_wait(barrier, n - 1)
    copies = []
    for j, peer in enumerate(peers):
        copies.append(
            pltpu.make_async_remote_copy(
                src_ref=partial,
                dst_ref=held.at[j],
                send_sem=send.at[j],
                recv_sem=recv.at[j],
                device_id={"date": peer},
                device_id_type=MESH,
            )
        )
        copies[-1].start()
    total = partial[...]
    for copy in copies:
        copy.wait_recv()
    for j in range(n - 1):
        total = total + held[j]
    rows = inverse.shape[0]
    for k in range(rows):
        value = jnp.sum(inverse[k] * total[k:k + 1], axis=1)[None]
        chips = series_out.shape[1]
        series_out[k // chips, k % chips:k % chips + 1] = value
    for copy in copies:
        copy.wait_send()


def body(n, strips, images, inverse, first, block, second, count, shifts, anchors):
    dates, length, cols = images.shape
    pairs, chips = first.shape[0], anchors.shape[0]
    vmem, smem = pl.BlockSpec(memory_space=pltpu.VMEM), pl.BlockSpec(memory_space=pltpu.SMEM)
    top = images[:, :SMAX].reshape(dates * SMAX, cols)
    bot = images[:, length - SMAX:].reshape(dates * SMAX, cols)
    tables = make_tables(length)
    kinds = 30 if n == 8 else 2 * n
    grid, halo = pl.pallas_call(
        functools.partial(gather_kernel, n, strips),
        name="gather",
        out_shape=(
            jax.ShapeDtypeStruct((n, dates, length, cols), BF16),
            jax.ShapeDtypeStruct((n, 2, dates * SMAX, cols), BF16),
        ),
        in_specs=[vmem] * 3,
        out_specs=(vmem, vmem),
        scratch_shapes=[
            pltpu.SemaphoreType.DMA((1,)),
            pltpu.SemaphoreType.DMA((kinds,)),
            pltpu.SemaphoreType.DMA((kinds,)),
        ],
        compiler_params=pltpu.CompilerParams(collective_id=0, has_side_effects=True),
    )(images, top, bot)
    width = 2 * length
    batch = 4
    offsets, partial = pl.pallas_call(
        functools.partial(pairs_kernel, n, strips, batch),
        name="pairs",
        out_shape=(
            jax.ShapeDtypeStruct((2, chips, pairs), F32),
            jax.ShapeDtypeStruct((2 * chips, n * dates), F32),
        ),
        in_specs=[smem] * 6 + [vmem] * 7,
        out_specs=(vmem, vmem),
        scratch_shapes=[
            pltpu.VMEM((pairs, length + 2 * SMAX, cols), F32),
            pltpu.VMEM((pairs * chips, length, cols), BF16),
            pltpu.VMEM((dates * chips, length, cols), BF16),
            pltpu.VMEM((dates * chips, length, 2 * width), BF16),
            pltpu.VMEM((chips, pairs, width), F32),
            pltpu.VMEM((chips, pairs, width), F32),
            pltpu.VMEM((pairs, cols), F32),
        ],
    )(
        first, block.reshape(pairs), second, count, jnp.transpose(shifts, (1, 2, 0)), anchors,
        images,
        grid.reshape(n * dates, length, cols),
        halo.reshape(n * dates, 2 * SMAX, cols),
        *tables,
    )
    share = inverse.shape[2]
    series = pl.pallas_call(
        functools.partial(series_kernel, n),
        name="series",
        out_shape=jax.ShapeDtypeStruct((2, chips, share), F32),
        in_specs=[vmem, vmem],
        out_specs=vmem,
        scratch_shapes=[
            pltpu.VMEM((n - 1, 2 * chips, n * dates), F32),
            pltpu.SemaphoreType.DMA((n - 1,)),
            pltpu.SemaphoreType.DMA((n - 1,)),
        ],
        compiler_params=pltpu.CompilerParams(collective_id=1, has_side_effects=True),
    )(partial, inverse.reshape(2 * chips, share, n * dates))
    return jnp.transpose(offsets, (2, 0, 1)), series


def solution(mesh):
    return jax.shard_map(
        functools.partial(body, mesh.shape["date"], mesh.shape["strip"]),
        mesh=mesh,
        in_specs=(
            P("date", "strip", None),
            P(None, "strip", "date", None),
            P("date"),
            P("date", None),
            P("date"),
            P("date"),
            P("date", None, "strip"),
            P("strip"),
        ),
        out_specs=(P("date", None, "strip"), P(None, "strip", "date")),
        check_vma=False,
    )
```

time: 85.4 us -> 46.7 us (0.55)
  Pallas kernels: 0 us -> 42.4 us
  waiting for transfers between devices: 17.5 us -> 0 us
  starting transfers between devices: 14.4 us -> 0 us
  blocking collectives: 11.8 us -> 0 us
  other arithmetic: 11.2 us -> 0 us
  matrix products: 9.92 us -> 0 us
  local copies, waits for them, and re-layouts: 11.9 us -> 2.65 us
  between operations: 8.17 us -> 1.29 us
    pallas_call x0 -> x3, Pallas kernels: none -> 42.4 us  [the longest x1 24 us: body(): pl.pallas_call(functools.partial(gather_kernel, n, strips), name='gather'...]
    all_to_all x2 -> x0, waiting for transfers between devices: 14.8 us -> none  [the longest x1 14.8 us: body(): lax.all_to_all(picked, 'date', split_axis=0, concat_axis=0, tiled=True)]
    psum x1 -> x0, blocking collectives: 11.8 us -> none  [body(): rhs_whole = lax.psum(partial_value, 'date')]
    dot_general x12 -> x0, matrix products: 9.92 us -> none  [the longest x1 2.75 us: one_turn(): jnp.einsum('pcif,pcfj->pcij', row_cut, col_pick, preferred_element_type=j...]
    all_to_all x2 -> x0, starting transfers between devices: 9.4 us -> none  [the longest x1 5.2 us: body(): lax.all_to_all(requests, 'date', split_axis=0, concat_axis=0, tiled=True)]
    another operation x7 -> x0, other arithmetic: 5.41 us -> none
    gather x3 -> x0, local copies, waits for them, and re-layouts: 5.04 us -> none  [the longest x1 3.54 us: one_turn(): regions_turn = jnp.take(regions, slots_turn, axis=0)]
    ppermute x2 -> x0, starting transfers between devices: 4.97 us -> none  [the longest x1 3.49 us: padded(): lax.ppermute(tail, axis, [(i, (i + 1) % count) for i in range(ends)])]
  transfers between devices with their start and end apart: 4 -> 0, of which waited for: 2 -> 0; matrix products, arithmetic and copies ran while one was open for 8% -> 0% of each run, Pallas kernels for 0% -> 0%
where the time goes in v1:
time: 46.7 us; the launch traced here: 46.4 us
  Pallas kernels  42.4 us (91%)
  local copies, waits for them, and re-layouts  2.65 us (6%)
  between operations  1.29 us (3%)
    pallas_call x1, Pallas kernels, body(): pl.pallas_call(functools.partial(gather_kernel, n, strips), name='gather'...  24 us
    pallas_call x1, Pallas kernels, body(): pl.pallas_call(functools.partial(pairs_kernel, n, strips, batch), name='p...  12.4 us
    pallas_call x1, Pallas kernels, body(): pl.pallas_call(functools.partial(series_kernel, n), name='series', out_sh...  6.07 us
    reshape x1, local copies, waits for them, and re-layouts, body(): bot = images[:, length - SMAX:].reshape(dates * SMAX, cols)  1.41 us
    unnamed x1, local copies, waits for them, and re-layouts  1.25 us

profile of v1, /device:TPU:0, one launch (start us, length us, event | category | flops | bytes accessed | tf_op | source)
XLA Modules:
  0.0 46.4 jit_solution(6920925273783579495)
XLA Ops:
  0.6 1.4 %slice_bitcast_fusion = (bf16[128,128]{1,0:T(8,128)(2,1)}, bf16[128,128]{1,0:T(8,128)(2,1)}) fusion(bf16[16,64,128]{2,1,0:T(8,128)(2,1)} %img.3), kind=kLoop, calls=%fused_computation | loop fusion | bytes 131072 | tf_op jit(solution)/shard_map/reshape | solution.py:339
  2.0 24.0 %gather.1 = (bf16[8,16,64,128]{3,2,1,0:T(8,128)(2,1)}, bf16[8,2,128,128]{3,2,1,0:T(8,128)(2,1)}) custom-call(bf16[16,64,128]{2,1,0:T(8,128)(2,1)} %img.3, bf16[128,128]{1,0:T(8,128)(2,1)} %get-tuple-element.11.top, bf16[128,128]{1,0:T(8,128)(2,1)} %get-tuple-element.10.bot), custom_call_target="tpu_custom_call" | custom-call | tf_op jit(solution)/shard_map/gather/pallas_call | solution.py:342
  26.7 12.4 %pairs.1 = (f32[2,2,32]{2,1,0:T(2,128)}, f32[4,128]{1,0:T(4,128)}) custom-call(s32[32]{0:T(128)} %first_s.1, s32[32]{0:T(128)} %bitcast.14, s32[32]{0:T(128)} %second_s.1, s32[1]{0:T(128)S(6)} %copy.15.count_s, s32[2,2,32]{2,1,0:T(2,128)} %bitcast.13, s32[2]{0:T(128)} %anchors_s.1, bf16[16,64,128]{2,1,0:T(8,128)(2,1)} %img.3, ...), custom_call_target="tpu_custom_call" | custom-call | tf_op jit(solution)/shard_map/pairs/pallas_call | solution.py:360
  39.1 6.1 %series.1 = f32[2,2,16]{2,1,0:T(2,128)} custom-call(f32[4,128]{1,0:T(4,128)} %get-tuple-element.9.partial, f32[4,16,128]{2,1,0:T(8,128)} %bitcast.12), custom_call_target="tpu_custom_call" | custom-call | tf_op jit(solution)/shard_map/series/pallas_call | solution.py:386
  45.1 1.2 %copy.16 = f32[2,2,16]{2,1,0:T(2,128)} copy(f32[2,2,16]{2,1,0:T(2,128)} %series.1) | data formatting | bytes 512

commit v2 on v1

--- a/solution.py
+++ b/solution.py
@@ -33,12 +33,13 @@
     return [jnp.asarray(t.astype(np.float32)).astype(BF16) for t in (forward, rows, back, final)]
 
 
-def gather_kernel(n, strips, img, top, bot, grid_out, halo_out, local, send, recv):
-    me = lax.axis_index("date")
-    strip = lax.axis_index("strip")
+def exchange(n, strips, img, grid, halo, local, send, recv):
+    me, strip = lax.axis_index("date"), lax.axis_index("strip")
     up, down = lax.rem(strip + strips - 1, strips), lax.rem(strip + 1, strips)
-    half = img.shape[0] // 2
-    first, second = pl.ds(0, half), pl.ds(half, img.shape[0] - half)
+    dates, length = img.shape[:2]
+    half = dates // 2
+    first, second = pl.ds(0, half), pl.ds(half, dates - half)
+    peers = [lax.rem(me + j, n) for j in range(1, n)]
 
     def sent(k, src, dst, where):
         return pltpu.make_async_remote_copy(
@@ -50,41 +51,39 @@
             device_id_type=MESH,
         )
 
-    hier = n == 8
-    if hier:
-        steps = [1, 2, 4]
-        peers = [jnp.bitwise_xor(me, j) for j in steps]
-    else:
-        peers = [lax.rem(me + j, n) for j in range(1, n)]
     barrier = pltpu.get_barrier_semaphore()
     for peer in peers:
         pl.semaphore_signal(barrier, inc=1, device_id={"date": peer}, device_id_type=MESH)
     for other in (up, down):
         pl.semaphore_signal(barrier, inc=1, device_id={"strip": other}, device_id_type=MESH)
-    own = pltpu.make_async_copy(img, grid_out.at[me], local.at[0])
+    own = pltpu.make_async_copy(img, grid.at[me], local.at[0])
     own.start()
-    pl.semaphore_wait(barrier, len(peers) + 2)
-
-    z_up = sent(0, top, halo_out.at[me, 0], {"strip": up})
-    z_down = sent(1, bot, halo_out.at[me, 1], {"strip": down})
-    if not hier:
+    pl.semaphore_wait(barrier, n + 1)
+
+    top, bot = img.at[:, pl.ds(0, SMAX)], img.at[:, pl.ds(length - SMAX, SMAX)]
+    z_up = sent(0, top, halo.at[me, 0], {"strip": up})
+    z_down = sent(1, bot, halo.at[me, 1], {"strip": down})
+    if n != 8:
         z_up.start()
         z_down.start()
-        mains = []
+        copies = []
         for j, peer in enumerate(peers):
-            mains.append(sent(2 + j, img, grid_out.at[me], {"date": peer}))
-            mains[-1].start()
+            copies.append(sent(2 + j, img, grid.at[me], {"date": peer}))
+            copies[-1].start()
         z_up.wait()
         z_down.wait()
         for j, peer in enumerate(peers):
-            mains.append(sent(n + 1 + j, halo_out.at[me], halo_out.at[me], {"date": peer}))
-            mains[-1].start()
-        for copy in mains:
+            copies.append(sent(n + 1 + j, halo.at[me], halo.at[me], {"date": peer}))
+            copies[-1].start()
+        yield
+        yield
+        yield
+        for copy in copies:
             copy.wait()
         own.wait()
         return
 
-    core, ex, wy = ({"date": peer} for peer in peers)
+    core, ex, wy = ({"date": jnp.bitwise_xor(me, j)} for j in (1, 2, 4))
 
     def family(base, own_ref, out, one, two):
         def made(k, block, part, where, mine=False):
@@ -109,8 +108,8 @@
             made(13, me, two, core, True),
         ]
 
-    main = family(2, img, grid_out, first, second)
-    halo = family(16, halo_out.at[me], halo_out, 0, 1)
+    main = family(2, img, grid, first, second)
+    edge = family(16, halo.at[me], halo, 0, 1)
 
     def run(copies, ids):
         for k in ids:
@@ -120,37 +119,40 @@
     z_up.start()
     z_down.start()
     run(main, (1, 3, 4, 13))
+    yield
+    z_up.wait_recv()
+    z_down.wait_recv()
+    run(edge, (0, 2, 1, 3, 4, 13))
     main[0].wait_recv()
     run(main, (5, 6))
     main[2].wait_recv()
     run(main, (7, 8))
-    z_up.wait_recv()
-    z_down.wait_recv()
-    run(halo, (0, 2, 1, 3, 4, 13))
+    yield
     main[1].wait_recv()
     run(main, (9,))
     main[3].wait_recv()
     run(main, (10,))
+    edge[0].wait_recv()
+    run(edge, (5, 6))
+    edge[2].wait_recv()
+    run(edge, (7, 8))
+    edge[1].wait_recv()
+    run(edge, (9,))
+    edge[3].wait_recv()
+    run(edge, (10,))
+    yield
     main[5].wait_recv()
     run(main, (11,))
     main[7].wait_recv()
     run(main, (12,))
-    halo[0].wait_recv()
-    run(halo, (5, 6))
-    halo[2].wait_recv()
-    run(halo, (7, 8))
-    halo[1].wait_recv()
-    run(halo, (9,))
-    halo[3].wait_recv()
-    run(halo, (10,))
-    halo[5].wait_recv()
-    run(halo, (11,))
-    halo[7].wait_recv()
-    run(halo, (12,))
+    edge[5].wait_recv()
+    run(edge, (11,))
+    edge[7].wait_recv()
+    run(edge, (12,))
     for k in (4, 13, 6, 8, 9, 10, 11, 12):
         main[k].wait_recv()
-        halo[k].wait_recv()
-    for copy in main + halo + [z_up, z_down]:
+        edge[k].wait_recv()
+    for copy in main + edge + [z_up, z_down]:
         copy.wait_send()
     own.wait()
 
@@ -158,8 +160,9 @@
 def pairs_kernel(
     n, strips, batch,
     first_s, block_s, second_s, count_s, shifts_s, anchors_s,
-    img, grid_in, halo_in, forward, rows, back, final,
-    offsets_out, partial_out,
+    img, forward, rows, back, final,
+    offsets_out, total_out,
+    grid_in, halo_in, partial, held_sums, local, send, recv,
     wide, far, near, spec, sums, moments, moves,
 ):
     dates, length, cols = img.shape
@@ -167,7 +170,8 @@
     me, strip = lax.axis_index("date"), lax.axis_index("strip")
     lane = lax.broadcasted_iota(jnp.int32, (length, cols), 1)
     has_up, has_down = strip > 0, strip < strips - 1
-    half_dates = dates // 2
+    moving = exchange(n, strips, img, grid_in, halo_in, local, send, recv)
+    next(moving)
 
     def turned(value, start):
         rolled = pltpu.roll(value, lax.rem(2 * cols - start, cols), 1)
@@ -184,12 +188,9 @@
 
     def far_cut(p, carry):
         block, day = block_s[p], second_s[p]
-        wide[p, pl.ds(SMAX, length)] = grid_in[block * dates + day].astype(F32)
-        odd = lax.rem(day, 2) == 1
-        tile = block * dates + day // 2
+        wide[p, pl.ds(SMAX, length)] = grid_in[block, day].astype(F32)
         for side, at, has in ((0, SMAX + length, has_down), (1, 0, has_up)):
-            held = halo_in[tile + side * half_dates].astype(F32)
-            edge = jnp.where(odd, held[SMAX:], held[:SMAX])
+            edge = halo_in[block, side, day].astype(F32)
             wide[p, pl.ds(at, SMAX)] = jnp.where(has, edge, 0.0)
         for c in range(chips):
             value = wide[p, pl.ds(SMAX + shifts_s[0, c, p], length)]
@@ -204,8 +205,6 @@
         moves[pl.ds(p, 1)] = row
         return carry
 
-    lax.fori_loop(0, pairs, far_cut, 0, unroll=4)
-
     width = 2 * length
     lanes2 = lax.broadcasted_iota(jnp.int32, (1, 2 * width), 1)
     base = jnp.where((lanes2 == 0) | (lanes2 == width + length), 1.0 / length, 0.0)
@@ -232,7 +231,14 @@
             spec[t * many + w] = both.astype(BF16)
         return carry
 
-    lax.fori_loop(0, dates // batch, near_turn, 0)
+    rounds = dates // batch
+    next(moving)
+    lax.fori_loop(0, rounds // 2, near_turn, 0)
+    next(moving)
+    lax.fori_loop(rounds // 2, rounds, near_turn, 0)
+    for _ in moving:
+        pass
+    lax.fori_loop(0, pairs, far_cut, 0, unroll=4)
 
     steps = lax.broadcasted_iota(jnp.int32, (width, 1), 0)
     down_k = jnp.where(steps < length, steps, steps - width).astype(F32) * 0.5
@@ -274,7 +280,7 @@
     live = lax.broadcasted_iota(jnp.int32, (pairs, 1), 0) < count_s[0]
     cells = 1.0 / (width * width)
     shift_all = moves[...]
-    spot = lax.broadcasted_iota(jnp.int32, (pairs, partial_out.shape[1]), 1).astype(F32)
+    spot = lax.broadcasted_iota(jnp.int32, (pairs, partial.shape[1]), 1).astype(F32)
     spread = (spot == shift_all[:, 2 * chips:2 * chips + 1]).astype(F32) - (
         spot == shift_all[:, 2 * chips + 1:2 * chips + 2]
     ).astype(F32)
@@ -291,82 +297,67 @@
     table = jnp.zeros((pairs, width), F32)
     for k, column in enumerate(columns):
         table = jnp.where(place == k, column, table)
-        partial_out[k:k + 1] = jnp.sum(column * spread, axis=0, keepdims=True)
+        partial[k:k + 1] = jnp.sum(column * spread, axis=0, keepdims=True)
     turned_table = jnp.transpose(table)
     for x in range(2):
         offsets_out[x] = turned_table[x * chips:(x + 1) * chips]
 
-
-def series_kernel(n, partial, inverse, series_out, held, send, recv):
-    me = lax.axis_index("date")
     peers = [lax.rem(me + j, n) for j in range(1, n)]
-    barrier = pltpu.get_barrier_semaphore()
-    for peer in peers:
-        pl.semaphore_signal(barrier, inc=1, device_id={"date": peer}, device_id_type=MESH)
-    pl.semaphore_wait(barrier, n - 1)
     copies = []
     for j, peer in enumerate(peers):
         copies.append(
             pltpu.make_async_remote_copy(
                 src_ref=partial,
-                dst_ref=held.at[j],
-                send_sem=send.at[j],
-                recv_sem=recv.at[j],
+                dst_ref=held_sums.at[j],
+                send_sem=send.at[send.shape[0] - n + 1 + j],
+                recv_sem=recv.at[recv.shape[0] - n + 1 + j],
                 device_id={"date": peer},
                 device_id_type=MESH,
             )
         )
         copies[-1].start()
     total = partial[...]
-    for copy in copies:
+    for j, copy in enumerate(copies):
         copy.wait_recv()
-    for j in range(n - 1):
-        total = total + held[j]
-    rows = inverse.shape[0]
-    for k in range(rows):
-        value = jnp.sum(inverse[k] * total[k:k + 1], axis=1)[None]
-        chips = series_out.shape[1]
-        series_out[k // chips, k % chips:k % chips + 1] = value
+        total = total + held_sums[j]
+    total_out[...] = total
     for copy in copies:
         copy.wait_send()
+
+
+def series_kernel(total, inverse, offsets, series_out, offsets_out):
+    offsets_out[...] = offsets[...]
+    chips = series_out.shape[1]
+    for k in range(inverse.shape[0]):
+        value = jnp.sum(inverse[k] * total[k:k + 1], axis=1)[None]
+        series_out[k // chips, k % chips:k % chips + 1] = value
 
 
 def body(n, strips, images, inverse, first, block, second, count, shifts, anchors):
     dates, length, cols = images.shape
     pairs, chips = first.shape[0], anchors.shape[0]
     vmem, smem = pl.BlockSpec(memory_space=pltpu.VMEM), pl.BlockSpec(memory_space=pltpu.SMEM)
-    top = images[:, :SMAX].reshape(dates * SMAX, cols)
-    bot = images[:, length - SMAX:].reshape(dates * SMAX, cols)
     tables = make_tables(length)
-    kinds = 30 if n == 8 else 2 * n
-    grid, halo = pl.pallas_call(
-        functools.partial(gather_kernel, n, strips),
-        name="gather",
-        out_shape=(
-            jax.ShapeDtypeStruct((n, dates, length, cols), BF16),
-            jax.ShapeDtypeStruct((n, 2, dates * SMAX, cols), BF16),
-        ),
-        in_specs=[vmem] * 3,
-        out_specs=(vmem, vmem),
-        scratch_shapes=[
-            pltpu.SemaphoreType.DMA((1,)),
-            pltpu.SemaphoreType.DMA((kinds,)),
-            pltpu.SemaphoreType.DMA((kinds,)),
-        ],
-        compiler_params=pltpu.CompilerParams(collective_id=0, has_side_effects=True),
-    )(images, top, bot)
+    kinds = (30 if n == 8 else 2 * n) + n - 1
     width = 2 * length
     batch = 4
-    offsets, partial = pl.pallas_call(
+    offsets, total = pl.pallas_call(
         functools.partial(pairs_kernel, n, strips, batch),
         name="pairs",
         out_shape=(
             jax.ShapeDtypeStruct((2, chips, pairs), F32),
             jax.ShapeDtypeStruct((2 * chips, n * dates), F32),
         ),
-        in_specs=[smem] * 6 + [vmem] * 7,
+        in_specs=[smem] * 6 + [vmem] * 5,
         out_specs=(vmem, vmem),
         scratch_shapes=[
+            pltpu.VMEM((n, dates, length, cols), BF16),
+            pltpu.VMEM((n, 2, dates, SMAX, cols), BF16),
+            pltpu.VMEM((2 * chips, n * dates), F32),
+            pltpu.VMEM((n - 1, 2 * chips, n * dates), F32),
+            pltpu.SemaphoreType.DMA((1,)),
+            pltpu.SemaphoreType.DMA((kinds,)),
+            pltpu.SemaphoreType.DMA((kinds,)),
             pltpu.VMEM((pairs, length + 2 * SMAX, cols), F32),
             pltpu.VMEM((pairs * chips, length, cols), BF16),
             pltpu.VMEM((dates * chips, length, cols), BF16),
@@ -375,27 +366,22 @@
             pltpu.VMEM((chips, pairs, width), F32),
             pltpu.VMEM((pairs, cols), F32),
         ],
+        compiler_params=pltpu.CompilerParams(collective_id=0, has_side_effects=True),
     )(
         first, block.reshape(pairs), second, count, jnp.transpose(shifts, (1, 2, 0)), anchors,
-        images,
-        grid.reshape(n * dates, length, cols),
-        halo.reshape(n * dates, 2 * SMAX, cols),
-        *tables,
+        images, *tables,
     )
     share = inverse.shape[2]
-    series = pl.pallas_call(
-        functools.partial(series_kernel, n),
+    series, offsets = pl.pallas_call(
+        series_kernel,
         name="series",
-        out_shape=jax.ShapeDtypeStruct((2, chips, share), F32),
-        in_specs=[vmem, vmem],
-        out_specs=vmem,
-        scratch_shapes=[
-            pltpu.VMEM((n - 1, 2 * chips, n * dates), F32),
-            pltpu.SemaphoreType.DMA((n - 1,)),
-            pltpu.SemaphoreType.DMA((n - 1,)),
-        ],
-        compiler_params=pltpu.CompilerParams(collective_id=1, has_side_effects=True),
-    )(partial, inverse.reshape(2 * chips, share, n * dates))
+        out_shape=(
+            jax.ShapeDtypeStruct((2, chips, share), F32),
+            jax.ShapeDtypeStruct((2, chips, pairs), F32),
+        ),
+        in_specs=[vmem] * 3,
+        out_specs=(vmem, vmem),
+    )(total, inverse.reshape(2 * chips, share, n * dates), offsets)
     return jnp.transpose(offsets, (2, 0, 1)), series
 
 

time: 46.7 us -> 34.5 us (0.74)
  Pallas kernels: 42.4 us -> 33 us
  local copies, waits for them, and re-layouts: 2.65 us -> 0 us
    pallas_call x2 -> x1, Pallas kernels: 30.1 us -> 1.43 us  [body(): pl.pallas_call(series_kernel, name='series', out_shape=(jax.ShapeDtypeStr...]
    pallas_call x1, Pallas kernels: 12.4 us -> 31.6 us  [body(): pl.pallas_call(functools.partial(pairs_kernel, n, strips, batch), name='p...]
    reshape x1 -> x0, local copies, waits for them, and re-layouts: 1.41 us -> none  [body(): bot = images[:, length - SMAX:].reshape(dates * SMAX, cols)]
    unnamed x1 -> x0, local copies, waits for them, and re-layouts: 1.25 us -> none
where the time goes in v2:
time: 34.5 us; the launch traced here: 34.3 us
  Pallas kernels  33 us (96%)
  between operations  1.29 us (4%)
    pallas_call x1, Pallas kernels, body(): pl.pallas_call(functools.partial(pairs_kernel, n, strips, batch), name='p...  31.6 us
    pallas_call x1, Pallas kernels, body(): pl.pallas_call(series_kernel, name='series', out_shape=(jax.ShapeDtypeStr...  1.43 us

profile of v2, /device:TPU:0, one launch (start us, length us, event | category | flops | bytes accessed | tf_op | source)
XLA Modules:
  0.0 34.3 jit_solution(4446675116012578516)
XLA Ops:
  1.3 31.6 %pairs.1 = (f32[2,2,32]{2,1,0:T(2,128)}, f32[4,128]{1,0:T(4,128)}) custom-call(s32[32]{0:T(128)} %first_s.1, s32[32]{0:T(128)} %bitcast.6, s32[32]{0:T(128)} %second_s.1, s32[1]{0:T(128)S(6)} %copy.14.count_s, s32[2,2,32]{2,1,0:T(2,128)} %bitcast.5, s32[2]{0:T(128)} %anchors_s.1, bf16[16,64,128]{2,1,0:T(8,128)(2,1)} %img.1, ...), custom_call_target="tpu_custom_call" | custom-call | tf_op jit(solution)/shard_map/pairs/pallas_call | solution.py:344
  32.8 1.4 %series.1 = (f32[2,2,16]{2,1,0:T(2,128)}, f32[2,2,32]{2,1,0:T(2,128)}) custom-call(f32[4,128]{1,0:T(4,128)} %get-tuple-element.6.total, f32[4,16,128]{2,1,0:T(8,128)} %bitcast.4, f32[2,2,32]{2,1,0:T(2,128)} %get-tuple-element.7.offsets), custom_call_target="tpu_custom_call" | custom-call | tf_op jit(solution)/shard_map/series/pallas_call | solution.py:375

commit v3 on v2

--- a/solution.py
+++ b/solution.py
@@ -33,13 +33,17 @@
     return [jnp.asarray(t.astype(np.float32)).astype(BF16) for t in (forward, rows, back, final)]
 
 
-def exchange(n, strips, img, grid, halo, local, send, recv):
+def exchange(n, strips, img, tables, grid, halo, local, send, recv):
     me, strip = lax.axis_index("date"), lax.axis_index("strip")
-    up, down = lax.rem(strip + strips - 1, strips), lax.rem(strip + 1, strips)
-    dates, length = img.shape[:2]
+    up, down = lax.max(strip - 1, 0), lax.min(strip + 1, strips - 1)
+    dates, length = grid.shape[1:3]
     half = dates // 2
     first, second = pl.ds(0, half), pl.ds(half, dates - half)
-    peers = [lax.rem(me + j, n) for j in range(1, n)]
+    if n == 8:
+        peers = [jnp.bitwise_xor(me, j) for j in (1, 2, 4)]
+    else:
+        peers = [lax.rem(me + j, n) for j in range(1, n)]
+    has_up, has_down = strip > 0, strip < strips - 1
 
     def sent(k, src, dst, where):
         return pltpu.make_async_remote_copy(
@@ -54,33 +58,59 @@
     barrier = pltpu.get_barrier_semaphore()
     for peer in peers:
         pl.semaphore_signal(barrier, inc=1, device_id={"date": peer}, device_id_type=MESH)
-    for other in (up, down):
-        pl.semaphore_signal(barrier, inc=1, device_id={"strip": other}, device_id_type=MESH)
+    for other, has in ((up, has_up), (down, has_down)):
+        @pl.when(has)
+        def _():
+            pl.semaphore_signal(barrier, inc=1, device_id={"strip": other}, device_id_type=MESH)
     own = pltpu.make_async_copy(img, grid.at[me], local.at[0])
     own.start()
-    pl.semaphore_wait(barrier, n + 1)
+    loads = [pltpu.make_async_copy(a, b, local.at[1 + k]) for k, (a, b) in enumerate(tables)]
+    for load in loads:
+        load.start()
+    for side, has in ((0, has_down), (1, has_up)):
+        @pl.when(jnp.logical_not(has))
+        def _():
+            halo[me, side] = jnp.zeros(halo.shape[2:], halo.dtype)
+    pl.semaphore_wait(barrier, len(peers) + has_up.astype(jnp.int32) + has_down.astype(jnp.int32))
 
     top, bot = img.at[:, pl.ds(0, SMAX)], img.at[:, pl.ds(length - SMAX, SMAX)]
     z_up = sent(0, top, halo.at[me, 0], {"strip": up})
     z_down = sent(1, bot, halo.at[me, 1], {"strip": down})
+
+    def start_z():
+        pl.when(has_up)(z_up.start)
+        pl.when(has_down)(z_down.start)
+
+    def got_z():
+        pl.when(has_down)(z_up.wait_recv)
+        pl.when(has_up)(z_down.wait_recv)
+
+    def left_z():
+        pl.when(has_up)(z_up.wait_send)
+        pl.when(has_down)(z_down.wait_send)
+
+    def settle():
+        own.wait()
+        for load in loads:
+            load.wait()
+
     if n != 8:
-        z_up.start()
-        z_down.start()
+        start_z()
         copies = []
         for j, peer in enumerate(peers):
             copies.append(sent(2 + j, img, grid.at[me], {"date": peer}))
             copies[-1].start()
-        z_up.wait()
-        z_down.wait()
+        got_z()
+        left_z()
         for j, peer in enumerate(peers):
             copies.append(sent(n + 1 + j, halo.at[me], halo.at[me], {"date": peer}))
             copies[-1].start()
+        settle()
         yield
         yield
         yield
         for copy in copies:
             copy.wait()
-        own.wait()
         return
 
     core, ex, wy = ({"date": jnp.bitwise_xor(me, j)} for j in (1, 2, 4))
@@ -116,12 +146,11 @@
             copies[k].start()
 
     run(main, (0, 2))
-    z_up.start()
-    z_down.start()
+    start_z()
     run(main, (1, 3, 4, 13))
+    settle()
     yield
-    z_up.wait_recv()
-    z_down.wait_recv()
+    got_z()
     run(edge, (0, 2, 1, 3, 4, 13))
     main[0].wait_recv()
     run(main, (5, 6))
@@ -152,25 +181,26 @@
     for k in (4, 13, 6, 8, 9, 10, 11, 12):
         main[k].wait_recv()
         edge[k].wait_recv()
-    for copy in main + edge + [z_up, z_down]:
+    for copy in main + edge:
         copy.wait_send()
-    own.wait()
+    left_z()
 
 
 def pairs_kernel(
     n, strips, batch,
     first_s, block_s, second_s, count_s, shifts_s, anchors_s,
-    img, forward, rows, back, final,
+    img, forward_in, rows_in, back_in, final_in,
     offsets_out, total_out,
-    grid_in, halo_in, partial, held_sums, local, send, recv,
+    forward, rows, back, final, grid_in, halo_in, partial, held_sums, local, send, recv,
     wide, far, near, spec, sums, moments, moves,
 ):
-    dates, length, cols = img.shape
+    dates, length, cols = grid_in.shape[1:]
     pairs, chips = first_s.shape[0], anchors_s.shape[0]
     me, strip = lax.axis_index("date"), lax.axis_index("strip")
     lane = lax.broadcasted_iota(jnp.int32, (length, cols), 1)
     has_up, has_down = strip > 0, strip < strips - 1
-    moving = exchange(n, strips, img, grid_in, halo_in, local, send, recv)
+    tables = ((forward_in, forward), (rows_in, rows), (back_in, back), (final_in, final))
+    moving = exchange(n, strips, img, tables, grid_in, halo_in, local, send, recv)
     next(moving)
 
     def turned(value, start):
@@ -179,7 +209,7 @@
         return jnp.where(inside, rolled, 0.0).astype(BF16)
 
     def near_cut(d, carry):
-        value = img[d].astype(F32)
+        value = grid_in[me, d].astype(F32)
         for c in range(chips):
             near[d * chips + c] = turned(value, anchors_s[c])
         return carry
@@ -348,14 +378,15 @@
             jax.ShapeDtypeStruct((2, chips, pairs), F32),
             jax.ShapeDtypeStruct((2 * chips, n * dates), F32),
         ),
-        in_specs=[smem] * 6 + [vmem] * 5,
+        in_specs=[smem] * 6 + [pl.BlockSpec(memory_space=pl.ANY)] * 5,
         out_specs=(vmem, vmem),
         scratch_shapes=[
+            *[pltpu.VMEM(table.shape, BF16) for table in tables],
             pltpu.VMEM((n, dates, length, cols), BF16),
             pltpu.VMEM((n, 2, dates, SMAX, cols), BF16),
             pltpu.VMEM((2 * chips, n * dates), F32),
             pltpu.VMEM((n - 1, 2 * chips, n * dates), F32),
-            pltpu.SemaphoreType.DMA((1,)),
+            pltpu.SemaphoreType.DMA((1 + len(tables),)),
             pltpu.SemaphoreType.DMA((kinds,)),
             pltpu.SemaphoreType.DMA((kinds,)),
             pltpu.VMEM((pairs, length + 2 * SMAX, cols), F32),

time: 34.5 us -> 32.3 us (0.936)
  Pallas kernels: 33 us -> 30.8 us
    pallas_call x1, Pallas kernels: 31.6 us -> 29.4 us  [body(): pl.pallas_call(functools.partial(pairs_kernel, n, strips, batch), name='p...]
where the time goes in v3:
time: 32.3 us; the launch traced here: 32.1 us
  Pallas kernels  30.8 us (95%)
  between operations  1.29 us (4%)
    pallas_call x1, Pallas kernels, body(): pl.pallas_call(functools.partial(pairs_kernel, n, strips, batch), name='p...  29.4 us
    pallas_call x1, Pallas kernels, body(): pl.pallas_call(series_kernel, name='series', out_shape=(jax.ShapeDtypeStr...  1.43 us

profile of v3, /device:TPU:0, one launch (start us, length us, event | category | flops | bytes accessed | tf_op | source)
XLA Modules:
  0.0 32.1 jit_solution(7795351247080779694)
XLA Ops:
  1.3 29.4 %pairs.1 = (f32[2,2,32]{2,1,0:T(2,128)}, f32[4,128]{1,0:T(4,128)}) custom-call(s32[32]{0:T(128)} %first_s.1, s32[32]{0:T(128)} %bitcast.6, s32[32]{0:T(128)} %second_s.1, s32[1]{0:T(128)S(6)} %copy.14.count_s, s32[2,2,32]{2,1,0:T(2,128)} %bitcast.5, s32[2]{0:T(128)} %anchors_s.1, bf16[16,64,128]{2,1,0:T(8,128)(2,1)} %img.1, ...), custom_call_target="tpu_custom_call" | custom-call | tf_op jit(solution)/shard_map/pairs/pallas_call | solution.py:374
  30.7 1.4 %series.1 = (f32[2,2,16]{2,1,0:T(2,128)}, f32[2,2,32]{2,1,0:T(2,128)}) custom-call(f32[4,128]{1,0:T(4,128)} %get-tuple-element.6.total, f32[4,16,128]{2,1,0:T(8,128)} %bitcast.4, f32[2,2,32]{2,1,0:T(2,128)} %get-tuple-element.7.offsets), custom_call_target="tpu_custom_call" | custom-call | tf_op jit(solution)/shard_map/series/pallas_call | solution.py:406

commit v4 on v3

--- a/solution.py
+++ b/solution.py
@@ -214,7 +214,7 @@
             near[d * chips + c] = turned(value, anchors_s[c])
         return carry
 
-    lax.fori_loop(0, dates, near_cut, 0, unroll=4)
+    lax.fori_loop(0, dates, near_cut, 0, unroll=8)
 
     def far_cut(p, carry):
         block, day = block_s[p], second_s[p]
@@ -268,7 +268,7 @@
     lax.fori_loop(rounds // 2, rounds, near_turn, 0)
     for _ in moving:
         pass
-    lax.fori_loop(0, pairs, far_cut, 0, unroll=4)
+    lax.fori_loop(0, pairs, far_cut, 0, unroll=16)
 
     steps = lax.broadcasted_iota(jnp.int32, (width, 1), 0)
     down_k = jnp.where(steps < length, steps, steps - width).astype(F32) * 0.5
@@ -370,7 +370,7 @@
     tables = make_tables(length)
     kinds = (30 if n == 8 else 2 * n) + n - 1
     width = 2 * length
-    batch = 4
+    batch = math.gcd(16, math.gcd(pairs, dates))
     offsets, total = pl.pallas_call(
         functools.partial(pairs_kernel, n, strips, batch),
         name="pairs",

time: 32.3 us -> 29.2 us (0.904)
  Pallas kernels: 30.8 us -> 27.7 us
    pallas_call x1, Pallas kernels: 29.4 us -> 26.3 us  [body(): pl.pallas_call(functools.partial(pairs_kernel, n, strips, batch), name='p...]
where the time goes in v4:
time: 29.2 us; the launch traced here: 29 us
  Pallas kernels  27.7 us (95%)
  between operations  1.29 us (4%)
    pallas_call x1, Pallas kernels, body(): pl.pallas_call(functools.partial(pairs_kernel, n, strips, batch), name='p...  26.3 us
    pallas_call x1, Pallas kernels, body(): pl.pallas_call(series_kernel, name='series', out_shape=(jax.ShapeDtypeStr...  1.43 us

profile of v4, /device:TPU:0, one launch (start us, length us, event | category | flops | bytes accessed | tf_op | source)
XLA Modules:
  0.0 29.0 jit_solution(3941251697397775334)
XLA Ops:
  1.3 26.3 %pairs.1 = (f32[2,2,32]{2,1,0:T(2,128)}, f32[4,128]{1,0:T(4,128)}) custom-call(s32[32]{0:T(128)} %first_s.1, s32[32]{0:T(128)} %bitcast.6, s32[32]{0:T(128)} %second_s.1, s32[1]{0:T(128)S(6)} %copy.14.count_s, s32[2,2,32]{2,1,0:T(2,128)} %bitcast.5, s32[2]{0:T(128)} %anchors_s.1, bf16[16,64,128]{2,1,0:T(8,128)(2,1)} %img.1, ...), custom_call_target="tpu_custom_call" | custom-call | tf_op jit(solution)/shard_map/pairs/pallas_call | solution.py:374
  27.6 1.4 %series.1 = (f32[2,2,16]{2,1,0:T(2,128)}, f32[2,2,32]{2,1,0:T(2,128)}) custom-call(f32[4,128]{1,0:T(4,128)} %get-tuple-element.6.total, f32[4,16,128]{2,1,0:T(8,128)} %bitcast.4, f32[2,2,32]{2,1,0:T(2,128)} %get-tuple-element.7.offsets), custom_call_target="tpu_custom_call" | custom-call | tf_op jit(solution)/shard_map/series/pallas_call | solution.py:406

commit v5 on v4

--- a/solution.py
+++ b/solution.py
@@ -268,7 +268,7 @@
     lax.fori_loop(rounds // 2, rounds, near_turn, 0)
     for _ in moving:
         pass
-    lax.fori_loop(0, pairs, far_cut, 0, unroll=16)
+    lax.fori_loop(0, pairs, far_cut, 0, unroll=32)
 
     steps = lax.broadcasted_iota(jnp.int32, (width, 1), 0)
     down_k = jnp.where(steps < length, steps, steps - width).astype(F32) * 0.5
@@ -303,7 +303,7 @@
                 moments[at] = jnp.sum(energy * down_k, axis=0, keepdims=True)
         return carry
 
-    lax.fori_loop(0, pairs // batch, turn, 0)
+    lax.fori_loop(0, pairs // batch, turn, 0, unroll=2)
 
     across = lax.broadcasted_iota(jnp.int32, (pairs, width), 1)
     across = jnp.where(across < length, across, across - width).astype(F32) * 0.5

time: 29.2 us -> 28.3 us (0.969)
  Pallas kernels: 27.7 us -> 26.8 us
    pallas_call x1, Pallas kernels: 26.3 us -> 25.4 us  [body(): pl.pallas_call(functools.partial(pairs_kernel, n, strips, batch), name='p...]
where the time goes in v5:
time: 28.3 us; the launch traced here: 28.1 us
  Pallas kernels  26.8 us (95%)
  between operations  1.29 us (5%)
    pallas_call x1, Pallas kernels, body(): pl.pallas_call(functools.partial(pairs_kernel, n, strips, batch), name='p...  25.4 us
    pallas_call x1, Pallas kernels, body(): pl.pallas_call(series_kernel, name='series', out_shape=(jax.ShapeDtypeStr...  1.43 us

profile of v5, /device:TPU:0, one launch (start us, length us, event | category | flops | bytes accessed | tf_op | source)
XLA Modules:
  0.0 28.1 jit_solution(4936734928309026987)
XLA Ops:
  1.3 25.4 %pairs.1 = (f32[2,2,32]{2,1,0:T(2,128)}, f32[4,128]{1,0:T(4,128)}) custom-call(s32[32]{0:T(128)} %first_s.1, s32[32]{0:T(128)} %bitcast.6, s32[32]{0:T(128)} %second_s.1, s32[1]{0:T(128)S(6)} %copy.14.count_s, s32[2,2,32]{2,1,0:T(2,128)} %bitcast.5, s32[2]{0:T(128)} %anchors_s.1, bf16[16,64,128]{2,1,0:T(8,128)(2,1)} %img.1, ...), custom_call_target="tpu_custom_call" | custom-call | tf_op jit(solution)/shard_map/pairs/pallas_call | solution.py:374
  26.7 1.4 %series.1 = (f32[2,2,16]{2,1,0:T(2,128)}, f32[2,2,32]{2,1,0:T(2,128)}) custom-call(f32[4,128]{1,0:T(4,128)} %get-tuple-element.6.total, f32[4,16,128]{2,1,0:T(8,128)} %bitcast.4, f32[2,2,32]{2,1,0:T(2,128)} %get-tuple-element.7.offsets), custom_call_target="tpu_custom_call" | custom-call | tf_op jit(solution)/shard_map/series/pallas_call | solution.py:406
